TPU v7x, 128 devices: a whole 4x4x4 slice. The times are simulated.
128 devices in a mesh: dp: 4 (over y), ctx: 32 (over x, z, core).
Axes of the slice: x: 4, y: 4, z: 4, core: 2. Of those that a mesh axis runs over, the one named last changes fastest.
Arguments:
- x_in: bfloat16 [4, 4096, 4096], P('dp', 'ctx'), may hold values from -6 to 6
- b_in: bfloat16 [4, 4096, 128], P('dp', 'ctx'), may hold values from -6 to 6
- c_in: bfloat16 [4, 4096, 128], P('dp', 'ctx'), may hold values from -6 to 6
- log_decay: int32 [4, 4096, 64], P('dp', 'ctx'), may hold values from 0 to 14000, as said below
- w_out: bfloat16 [4096, 2048], P(('dp', 'ctx')), may hold values from -0.09375 to 0.09375
- cotangent: bfloat16 [4, 4096, 2048], P('dp', 'ctx'), may hold values from -6 to 6
Outputs:
- out: bfloat16 [4, 4096, 2048], P('dp', 'ctx')
- grad_x: bfloat16 [4, 4096, 4096], P('dp', 'ctx')
- grad_b: bfloat16 [4, 4096, 128], P('dp', 'ctx')
- gradient_c_input: bfloat16 [4, 4096, 128], P('dp', 'ctx')
Inputs may be any that keep to these rules, and one draw needn't show every extreme that they name: log_decay holds each head's per-token log-decay as a whole number.
All inputs are finite; a program needn't handle non-finite values.
Results may differ from a plain program's by a relative error of at most 0.01.
Values may be sent and summed in bfloat16 or wider, within the bound.
A program may use at most 320 MiB of HBM per device.

v0:
```python
import jax
import jax.numpy as jnp
from jax import lax
from jax.sharding import PartitionSpec as P

decay_unit = 5e-05


def causal_decay(local_group):
    cum = local_group.T
    rows = cum.shape[1]
    diff = (cum[:, :, None] - cum[:, None, :]).astype(jnp.float32)
    lower = lax.broadcasted_iota(jnp.int32, (rows, rows), 0) >= lax.broadcasted_iota(
        jnp.int32, (rows, rows), 1
    )
    return jnp.where(lower[None], jnp.exp(-decay_unit * diff), jnp.float32(0.0))


def forward_inside_group(x_bf, local, scores, scale, group, width):
    rows, inner = x_bf.shape
    heads = local.shape[1]
    count = heads // group
    x_groups = x_bf.reshape(rows, count, group, width).transpose(1, 0, 2, 3)
    l_groups = local.reshape(rows, count, group).transpose(1, 0, 2)

    def forward_one_group(carry, item):
        x_part, l_part = item
        mix = (scale * scores[None] * causal_decay(l_part)).astype(jnp.bfloat16)
        part = jnp.einsum("gtr,rgp->tgp", mix, x_part, preferred_element_type=jnp.float32)
        return (carry, (mix, part))

    _, (mixes, parts) = lax.scan(
        forward_one_group, jnp.zeros((), jnp.float32), (x_groups, l_groups)
    )
    return (mixes, parts.transpose(1, 0, 2, 3).reshape(rows, inner))


def backward_intra(mixes, x_bf, back_bf, local, scale, group, width):
    rows, inner = x_bf.shape
    heads = local.shape[1]
    count = heads // group
    x_groups = x_bf.reshape(rows, count, group, width).transpose(1, 0, 2, 3)
    d_groups = back_bf.reshape(rows, count, group, width).transpose(1, 0, 2, 3)
    l_groups = local.reshape(rows, count, group).transpose(1, 0, 2)

    def backward_one_group(total, item):
        mix, x_part, d_part, l_part = item
        flowed = jnp.einsum("gtr,tgp->rgp", mix, d_part, preferred_element_type=jnp.float32)
        inner_prod = jnp.einsum("tgp,rgp->gtr", d_part, x_part, preferred_element_type=jnp.float32)
        total = total + jnp.sum(scale * causal_decay(l_part) * inner_prod, axis=0)
        return (total, flowed)

    kernel, flows = lax.scan(
        backward_one_group,
        jnp.zeros((rows, rows), jnp.float32),
        (mixes, x_groups, d_groups, l_groups),
    )
    return (kernel, flows.transpose(1, 0, 2, 3).reshape(rows, inner))


def body(x_in, b_in, c_in, log_decay, w_out, cotangent):
    x_bf = x_in[0]
    b_blk = b_in[0]
    c_blk = c_in[0]
    steps = log_decay[0]
    grad_out = cotangent[0]
    rows, inner = x_bf.shape
    heads = steps.shape[1]
    width = inner // heads
    length = rows * lax.axis_size("ctx")
    scale = (b_blk.shape[1] * length) ** (-0.5)
    group = 8
    local = jnp.cumsum(steps, axis=0)
    totals = local[-1]
    fall_wide = jnp.repeat(jnp.exp(-decay_unit * local.astype(jnp.float32)), width, axis=1)
    tail_wide = jnp.repeat(
        jnp.exp(-decay_unit * (totals[None, :] - local).astype(jnp.float32)), width, axis=1
    )
    scores = jnp.dot(c_blk, b_blk.T, preferred_element_type=jnp.float32)
    mixes, y_intra = forward_inside_group(x_bf, local, scores, scale, group, width)
    shifted = (x_bf * tail_wide).astype(jnp.bfloat16)
    term = jnp.dot(b_blk.T, shifted, preferred_element_type=jnp.float32)
    mine = lax.axis_index("ctx")
    all_totals = lax.all_gather(totals[None, :], "ctx", axis=0, tiled=True)
    before_sum = jnp.cumsum(all_totals, axis=0) - all_totals
    mine_before = lax.dynamic_slice_in_dim(before_sum, mine, 1, 0)
    mine_total = lax.dynamic_slice_in_dim(all_totals, mine, 1, 0)

    def weighted_add(carry, piece, later):
        count = piece.shape[0]
        index_set = jnp.arange(count, dtype=jnp.int32)
        if later:
            span = before_sum - mine_before - mine_total
            live = index_set > mine
        else:
            span = mine_before - before_sum - all_totals
            live = index_set < mine
        span = jnp.maximum(span, 0).astype(jnp.float32)
        weight = jnp.where(live[:, None], jnp.exp(-decay_unit * span), jnp.float32(0.0))
        weight_wide = jnp.repeat(weight, width, axis=1)
        return carry + jnp.einsum("ksi,ki->si", piece, weight_wide, precision=lax.Precision.HIGHEST)

    before = weighted_add(
        jnp.zeros_like(term), lax.all_gather(term[None], "ctx", axis=0, tiled=True), False
    )
    before_bf = before.astype(jnp.bfloat16)
    mixed = (
        y_intra + scale * fall_wide * jnp.dot(c_blk, before_bf, preferred_element_type=jnp.float32)
    ).astype(jnp.bfloat16)
    whole_proj = lax.all_gather(w_out, ("dp", "ctx"), axis=0, tiled=True)
    out = jnp.dot(mixed, whole_proj, preferred_element_type=jnp.float32).astype(jnp.bfloat16)
    back_bf = lax.dot_general(
        grad_out, whole_proj, (((1,), (1,)), ((), ())), preferred_element_type=jnp.float32
    ).astype(jnp.bfloat16)
    dshift = (back_bf * fall_wide).astype(jnp.bfloat16)
    adjoint_term = jnp.dot(c_blk.T, dshift, preferred_element_type=jnp.float32)
    after = weighted_add(
        jnp.zeros_like(adjoint_term),
        lax.all_gather(adjoint_term[None].astype(jnp.bfloat16), "ctx", axis=0, tiled=True).astype(
            jnp.float32
        ),
        True,
    )
    after_bf = after.astype(jnp.bfloat16)
    kernel, dx_intra = backward_intra(mixes, x_bf, back_bf, local, scale, group, width)
    kernel_bf = kernel.astype(jnp.bfloat16)
    grad_x = (
        dx_intra + scale * tail_wide * jnp.dot(b_blk, after_bf, preferred_element_type=jnp.float32)
    ).astype(jnp.bfloat16)
    grad_b = (
        jnp.dot(kernel_bf.T, c_blk, preferred_element_type=jnp.float32)
        + scale * jnp.dot(shifted, after_bf.T, preferred_element_type=jnp.float32)
    ).astype(jnp.bfloat16)
    gradient_c_input = (
        jnp.dot(kernel_bf, b_blk, preferred_element_type=jnp.float32)
        + scale * jnp.dot(dshift, before_bf.T, preferred_element_type=jnp.float32)
    ).astype(jnp.bfloat16)
    return (out[None], grad_x[None], grad_b[None], gradient_c_input[None])


def solution(mesh):
    in_specs = (
        P("dp", "ctx", None),
        P("dp", "ctx", None),
        P("dp", "ctx", None),
        P("dp", "ctx", None),
        P(("dp", "ctx"), None),
        P("dp", "ctx", None),
    )
    out_specs = (
        P("dp", "ctx", None),
        P("dp", "ctx", None),
        P("dp", "ctx", None),
        P("dp", "ctx", None),
    )
    return jax.shard_map(body, mesh=mesh, in_specs=in_specs, out_specs=out_specs, check_vma=False)
```

profile of v0, /device:TPU:1, one launch (start us, length us, event | category | flops | bytes accessed | tf_op | source)
XLA Modules:
  0.0 575.8 jit_solution(17110521173736781467)
XLA Ops:
  9.3 1.9 copy.35
  11.2 83.5 %all-gather.7.cloned.1.call-done = bf16[4096,2048]{1,0:T(8,128)(2,1)} async-done(((bf16[32,2048]{1,0:T(8,128)(2,1)}), bf16[4096,2048]{1,0:T(8,128)(2,1)}) %all-gather.7.cloned.1.call-update) | async-done | bytes 16777232 | tf_op jit(solution)/shard_map/all_gather | solution.py:110
  94.8 12.6 %convolution_convert_fusion = bf16[128,4096]{1,0:T(8,128)(2,1)} fusion(bf16[4096,2048]{1,0:T(8,128)(2,1)} %all-gather.7.cloned.1.call-done, bf16[1,128,2048]{2,1,0:T(8,128)(2,1)S(1)} %copy-done), kind=kOutput, calls=%fused_computation.43 | convolution fusion | flops 2148007936 | bytes 18350080 | tf_op jit(solution)/shard_map/dot_general | solution.py:112
  107.4 2.7 fusion.31
  114.0 1.9 fusion.34
  116.0 21.5 %all-gather.2 = s32[32,1,64]{2,1,0:T(1,128)S(1)} all-gather(s32[1,1,64]{2,1,0:T(1,128)S(1)} %get-tuple-element.140), channel_id=1, replica_groups=mesh['dp'=4,'ctx'=32] {'ctx'}, dimensions={0}, use_global_device_ids=true | all-gather | bytes 8448 | tf_op jit(solution)/shard_map/all_gather | solution.py:84
  139.7 16.4 %while.25 = (s32[]{:T(128)}, bf16[8,8,128,128]{3,2,1,0:T(8,128)(2,1)}, f32[8,128,8,64]{1,3,2,0:T(8,128)}, f32[128,128]{1,0:T(8,128)S(1)}, s32[8,128,8]{1,2,0:T(8...) while((s32[]{:T(128)}, bf16[8,8,128,128]{3,2,1,0:T(8,128)(2,1)}, f32[8,128,8,64]{1,3,2,0:T(8,128)}, ...), condition=%wide.region_2.3_spmd, body=%wide.region_1.2_spmd.sunk | while | flops 18382848 | bytes 992349 | solution.py:32
  159.0 26.1 %while.26 = (s32[]{:T(128)}, f32[128,128]{1,0:T(8,128)S(1)}, f32[8,128,8,64]{1,3,2,0:T(8,128)}, s32[8,128,8]{1,2,0:T(8,128)S(1)}, bf16[8,128,8,64]{1,3,2,0:T(8,1...) while((s32[]{:T(128)}, f32[128,128]{1,0:T(8,128)S(1)}, ...), condition=%wide.region_6.7_spmd.clone, body=%wide.region_4.6_spmd.clone.sunk | while | flops 34504704 | bytes 1231475 | solution.py:53
  160.3 2.0 fusion.90
  163.5 2.0 fusion.90
  166.8 1.9 fusion.90
  173.2 1.9 fusion.90
  176.5 1.9 fusion.90
  179.7 2.1 fusion.90
  183.1 2.0 fusion.90
  185.4 49.2 %all-gather.11.cloned.1.call-done = bf16[4096,4096]{0,1:T(8,128)(2,1)} async-done(((bf16[128,4096]{0,1:T(8,128)(2,1)}), bf16[4096,4096]{0,1:T(8,128)(2,1)}) %all-gather.11.cloned.1.call-update) | async-done | bytes 33554448 | tf_op jit(solution)/shard_map/all_gather | solution.py:119
  234.5 23.8 %copy.46 = bf16[512,8,32,128]{3,2,1,0:T(8,128)(2,1)} copy(bf16[512,8,32,128]{3,1,2,0:T(8,128)(2,1)} %bitcast.164) | data formatting | bytes 67108864
  258.5 29.8 %fusion.64 = f32[4096,1,128]{2,1,0:T(1,128)S(1)} fusion(f32[32,4096,1]{0,2,1:T(1,128)S(1)} %bitcast.179, bf16[32,128,4096]{1,0,2:T(8,128)(2,1)} %bitcast.165), kind=kOutput, calls=%fused_computation.95 | convolution fusion | flops 201326592 | bytes 36175872 | tf_op jit(solution)/shard_map/ksi,ki->si/dot_general | solution.py:101
  289.9 2.3 copy.36
  292.1 2.3 fusion.40
  294.4 159.6 %all-gather.9.cloned.1.call-done = f32[4096,4096]{0,1:T(8,128)} async-done(((f32[128,4096]{0,1:T(8,128)}), f32[4096,4096]{0,1:T(8,128)}) %all-gather.9.cloned.1.call-update) | async-done | bytes 67108880 | tf_op jit(solution)/shard_map/all_gather | solution.py:104
  454.0 44.1 %copy.45 = f32[512,8,32,128]{3,2,1,0:T(8,128)} copy(f32[512,8,32,128]{3,1,2,0:T(8,128)} %bitcast.60) | data formatting | bytes 134217728
  498.3 58.8 %fusion.63 = f32[4096,1,128]{2,1,0:T(1,128)S(1)} fusion(f32[32,4096,1]{0,2,1:T(1,128)S(1)} %bitcast.170, f32[32,128,4096]{1,0,2:T(8,128)} %bitcast.62), kind=kOutput, calls=%fused_computation.94 | convolution fusion | flops 201326592 | bytes 69730304 | tf_op jit(solution)/shard_map/ksi,ki->si/dot_general | solution.py:101
  558.3 11.0 %fusion.33 = bf16[1,128,2048]{2,1,0:T(8,128)(2,1)} fusion(bf16[4096,2048]{1,0:T(8,128)(2,1)} %all-gather.7.cloned.1.call-done, f32[128,4096]{0,1:T(8,128)} %bitcast.176, f32[128,4096]{0,1:T(8,128)} %bitcast.169, f32[4096,128]{1,0:T(8,128)S(1)} %bitcast.167, bf16[1,128,128]{2,1,0:T(8,128)(2,1)S(1)} %copy-done.10), kind=kOutput, calls=%fused_computation.52 | convolution fusion | flops 2284584960 | bytes 23625728 | tf_op jit(solution)/shard_map/dot_general | solution.py:111
  (132 shorter events, 42.7 us)
Async XLA Ops:
  7.2 87.6 %copy-start = (bf16[1,128,2048]{2,1,0:T(8,128)(2,1)S(1)}, bf16[1,128,2048]{2,1,0:T(8,128)(2,1)}, u32[]{:S(2)}) copy-start(bf16[1,128,2048]{2,1,0:T(8,128)(2,1)} %param.15) | copy-start | bytes 1572868
  7.2 87.6 %all-gather.7.cloned.1.call-start = ((), (), s32[]{:S(2)}) async-start(), calls=%async_computation | async-start | bytes 16908288 | tf_op jit(solution)/shard_map/all_gather | solution.py:110
  7.9 226.6 %all-gather.11.cloned.1.call-start = ((), (), s32[]{:S(2)}) async-start(), calls=%async_computation.2 | async-start | bytes 34603008 | tf_op jit(solution)/shard_map/all_gather | solution.py:119
  9.3 2.0 copy-start.2
  11.2 96.1 %copy-start.10 = (bf16[1,128,128]{2,1,0:T(8,128)(2,1)S(1)}, bf16[1,128,128]{2,1,0:T(8,128)(2,1)}, u32[]{:S(2)}) copy-start(bf16[1,128,128]{2,1,0:T(8,128)(2,1)} %param.12) | copy-start | bytes 98308
  94.8 12.6 %copy-start.3 = (f32[128,4096]{1,0:T(8,128)S(1)}, f32[128,4096]{1,0:T(8,128)}, u32[]{:S(2)}) copy-start(f32[128,4096]{1,0:T(8,128)} %copy.35) | copy-start | bytes 6291460
  110.1 343.9 %all-gather.9.cloned.1.call-start = ((), (), s32[]{:S(2)}) async-start(), calls=%async_computation.1 | async-start | bytes 69206016 | tf_op jit(solution)/shard_map/all_gather | solution.py:104
  110.2 2.0 copy-start.9
  139.7 16.4 %copy-start.5 = (bf16[128,4096]{1,0:T(8,128)(2,1)S(1)}, bf16[128,4096]{1,0:T(8,128)(2,1)}, u32[]{:S(2)}) copy-start(bf16[128,4096]{1,0:T(8,128)(2,1)} %convolution_convert_fusion) | copy-start | bytes 3145732
  258.5 29.8 %copy-start.7 = (f32[128,4096]{0,1:T(8,128)S(1)}, f32[128,4096]{0,1:T(8,128)}, u32[]{:S(2)}) copy-start(f32[128,4096]{0,1:T(8,128)} %get-tuple-element.142) | copy-start | bytes 6291460
  258.5 29.8 %copy-start.8 = (f32[8,128,8,64]{1,3,2,0:T(8,128)S(1)}, f32[8,128,8,64]{1,3,2,0:T(8,128)}, u32[]{:S(2)}) copy-start(f32[8,128,8,64]{1,3,2,0:T(8,128)} %get-tuple-element.77) | copy-start | bytes 6291460
  498.3 58.9 %copy-start.4 = (f32[128,4096]{1,0:T(8,128)S(1)}, f32[128,4096]{1,0:T(8,128)}, u32[]{:S(2)}) copy-start(f32[128,4096]{1,0:T(8,128)} %copy.35) | copy-start | bytes 6291460
  498.3 58.9 %copy-start.6 = (bf16[128,4096]{1,0:T(8,128)(2,1)S(1)}, bf16[128,4096]{1,0:T(8,128)(2,1)}, u32[]{:S(2)}) copy-start(bf16[128,4096]{1,0:T(8,128)(2,1)} %convolution_convert_fusion) | copy-start | bytes 3145732
  558.3 11.0 %copy-start.1 = (bf16[1,128,2048]{2,1,0:T(8,128)(2,1)S(1)}, bf16[1,128,2048]{2,1,0:T(8,128)(2,1)}, u32[]{:S(2)}) copy-start(bf16[1,128,2048]{2,1,0:T(8,128)(2,1)} %param.15) | copy-start | bytes 1572868
Sparse Core Ops, SparseCore 0:
  11.1 83.5 all-gather.6
  110.2 124.2 all-gather.10
  236.7 217.2 all-gather.8
where the time goes:
time: 576 us
  waiting for transfers between devices  293 us (51%)
  matrix products  156 us (27%)
  local copies, waits for them, and re-layouts  80.1 us (14%)
  blocking collectives  21.5 us (4%)
  between operations  14 us (2%)
  other arithmetic  10.4 us (2%)
    all_gather x1, waiting for transfers between devices, body(): lax.all_gather(term[None], 'ctx', axis=0, tiled=True)  160 us
    dot_general x2, matrix products, weighted_add(): jnp.einsum('ksi,ki->si', piece, weight_wide, precision=lax.Precision.HIGH...  88.7 us
    all_gather x1, waiting for transfers between devices, body(): whole_proj = lax.all_gather(w_out, ('dp', 'ctx'), axis=0, tiled=True)  83.5 us
    unnamed x28, local copies, waits for them, and re-layouts  72.1 us
    all_gather x1, waiting for transfers between devices, body(): lax.all_gather(adjoint_term[None].astype(jnp.bfloat16), 'ctx', axis=0, ti...  49.2 us
    all_gather x1, blocking collectives, body(): all_totals = lax.all_gather(totals[None, :], 'ctx', axis=0, tiled=True)  21.5 us
    dot_general x8, matrix products, backward_one_group(): jnp.einsum('gtr,tgp->rgp', mix, d_part, preferred_element_type=jnp.float32)  15.7 us
    dot_general x1, matrix products, body(): lax.dot_general(grad_out, whole_proj, (((1,), (1,)), ((), ())), preferred...  12.6 us
  transfers between devices with their start and end apart: 3, of which 3 were waited for; matrix products, arithmetic and copies ran while one was open for 20% of the time, Pallas kernels for 0%

commit v1 on v0

--- a/solution.py
+++ b/solution.py
@@ -1,9 +1,21 @@
+import functools
 import jax
 import jax.numpy as jnp
 from jax import lax
 from jax.sharding import PartitionSpec as P
+from jax.lax import all_to_all, axis_size
 
 decay_unit = 5e-05
+
+
+def sectors_recover(x_local, array_dim):
+    row_out = axis_size("ctx")
+    local_out = jnp.stack(row_out * [x_local], axis=0)
+    z_new = all_to_all(local_out, axis_name="ctx", split_axis=0, concat_axis=0)
+    return jnp.concatenate(z_new, array_dim)
+
+
+show_the_cube = functools.partial(sectors_recover, array_dim=0)
 
 
 def causal_decay(local_group):
@@ -100,9 +112,7 @@
         weight_wide = jnp.repeat(weight, width, axis=1)
         return carry + jnp.einsum("ksi,ki->si", piece, weight_wide, precision=lax.Precision.HIGHEST)
 
-    before = weighted_add(
-        jnp.zeros_like(term), lax.all_gather(term[None], "ctx", axis=0, tiled=True), False
-    )
+    before = weighted_add(jnp.zeros_like(term), show_the_cube(term[None]), False)
     before_bf = before.astype(jnp.bfloat16)
     mixed = (
         y_intra + scale * fall_wide * jnp.dot(c_blk, before_bf, preferred_element_type=jnp.float32)

time: 576 us -> 1420 us (2.47)
  waiting for transfers between devices: 293 us -> 750 us
  blocking collectives: 21.5 us -> 433 us
  matrix products: 156 us -> 107 us
  other arithmetic: 10.4 us -> 33.9 us
    all_gather x1, waiting for transfers between devices: 83.5 us -> 749 us  [body(): whole_proj = lax.all_gather(w_out, ('dp', 'ctx'), axis=0, tiled=True)]
    all_gather x1, blocking collectives: 21.5 us -> 433 us  [body(): all_totals = lax.all_gather(totals[None, :], 'ctx', axis=0, tiled=True)]
    all_gather x1 -> x0, waiting for transfers between devices: 160 us -> none  [body(): lax.all_gather(term[None], 'ctx', axis=0, tiled=True)]
    dot_general x2 -> x1, matrix products: 88.7 us -> 29.8 us  [weighted_add(): jnp.einsum('ksi,ki->si', piece, weight_wide, precision=lax.Precision.HIGH...]
    all_gather x1, waiting for transfers between devices: 49.2 us -> 0.01 us  [body(): lax.all_gather(adjoint_term[None].astype(jnp.bfloat16), 'ctx', axis=0, ti...]
    unnamed x28 -> x23, local copies, waits for them, and re-layouts: 72.1 us -> 28.5 us
    another operation x2 -> x3, local copies, waits for them, and re-layouts: 3.28 us -> 25.9 us  [the longest x1 22.7 us: sectors_recover(): local_out = jnp.stack(row_out * [x_local], axis=0)]
    unnamed x1 -> x2, other arithmetic: 0.01 us -> 22.3 us
  transfers between devices with their start and end apart: 3 -> 3, of which waited for: 3 -> 1; matrix products, arithmetic and copies ran while one was open for 20% -> 11% of each run, Pallas kernels for 0% -> 0%
where the time goes in v1:
time: 1420 us
  waiting for transfers between devices  750 us (53%)
  blocking collectives  433 us (30%)
  matrix products  107 us (8%)
  local copies, waits for them, and re-layouts  69.6 us (5%)
  other arithmetic  33.9 us (2%)
    all_gather x1, waiting for transfers between devices, body(): whole_proj = lax.all_gather(w_out, ('dp', 'ctx'), axis=0, tiled=True)  749 us
    all_gather x1, blocking collectives, body(): all_totals = lax.all_gather(totals[None, :], 'ctx', axis=0, tiled=True)  433 us
    dot_general x1, matrix products, weighted_add(): jnp.einsum('ksi,ki->si', piece, weight_wide, precision=lax.Precision.HIGH...  29.8 us
    unnamed x23, local copies, waits for them, and re-layouts  28.5 us
  transfers between devices with their start and end apart: 3, of which 1 were waited for; matrix products, arithmetic and copies ran while one was open for 11% of the time, Pallas kernels for 0%

profile of v1, /device:TPU:1, one launch (start us, length us, event | category | flops | bytes accessed | tf_op | source)
XLA Modules:
  0.0 1417.0 jit_solution(4171267866970410772)
XLA Ops:
  12.8 3.0 copy.36
  15.8 22.7 %stack.3 = f32[32,1,128,4096]{3,2,1,0:T(8,128)} broadcast(f32[128,4096]{1,0:T(8,128)} %copy.36), dimensions={2,3} | broadcast | bytes 69206016 | tf_op jit(solution)/shard_map/stack | solution.py:13
  38.5 9.5 all-to-all-start
  51.6 749.4 %all-gather.5.cloned.1.call-done = bf16[4096,2048]{1,0:T(8,128)(2,1)} async-done(((bf16[32,2048]{1,0:T(8,128)(2,1)}), bf16[4096,2048]{1,0:T(8,128)(2,1)}) %all-gather.5.cloned.1.call-update) | async-done | bytes 16777232 | tf_op jit(solution)/shard_map/all_gather | solution.py:120
  801.0 12.4 convolution_convert_fusion
  813.4 2.7 fusion.32
  816.2 3.2 fusion.35
  819.4 432.7 %all-gather.1 = s32[32,1,64]{2,1,0:T(1,128)S(1)} all-gather(s32[1,1,64]{2,1,0:T(1,128)S(1)} %get-tuple-element.137), channel_id=1, replica_groups=mesh['dp'=4,'ctx'=32] {'ctx'}, dimensions={0}, use_global_device_ids=true | all-gather | bytes 8448 | tf_op jit(solution)/shard_map/all_gather | solution.py:96
  1257.0 23.5 %while.25 = (s32[]{:T(128)}, bf16[8,8,128,128]{3,2,1,0:T(8,128)(2,1)}, f32[8,128,8,64]{1,3,2,0:T(8,128)}, f32[128,128]{1,0:T(8,128)S(1)}, s32[8,128,8]{1,2,0:T(8...) while((s32[]{:T(128)}, bf16[8,8,128,128]{3,2,1,0:T(8,128)(2,1)}, f32[8,128,8,64]{1,3,2,0:T(8,128)}, ...), condition=%wide.region_2.3_spmd, body=%wide.region_1.2_spmd.sunk | while | flops 18382848 | bytes 992849 | solution.py:44
  1257.0 2.0 fusion.84
  1260.0 2.0 fusion.84
  1271.7 2.0 fusion.84
  1274.7 2.0 fusion.84
  1277.6 2.0 fusion.84
  1280.5 2.3 copy.37
  1284.4 26.5 %while.26 = (s32[]{:T(128)}, f32[128,128]{1,0:T(8,128)S(1)}, f32[8,128,8,64]{1,3,2,0:T(8,128)}, s32[8,128,8]{1,2,0:T(8,128)S(1)}, bf16[8,128,8,64]{1,3,2,0:T(8,1...) while((s32[]{:T(128)}, f32[128,128]{1,0:T(8,128)S(1)}, ...), condition=%wide.region_6.7_spmd.clone, body=%wide.region_4.6_spmd.clone.sunk | while | flops 34504704 | bytes 1231467 | solution.py:65
  1311.2 22.2 %fusion.25 = bf16[4096,128]{0,1:T(8,128)(2,1)} fusion(f32[32,1,128,4096]{3,2,1,0:T(8,128)} %all-to-all-done, f32[4096,32]{0,1:T(8,128)S(1)} %bitcast.176), kind=kLoop, calls=%fused_computation.37 | loop fusion | flops 33030144 | bytes 68681728
  1333.5 2.3 copy.46
  1335.7 2.6 fusion.40
  1338.3 11.2 fusion.34
  1349.5 23.0 %copy.52 = bf16[512,8,32,128]{3,2,1,0:T(8,128)(2,1)} copy(bf16[512,8,32,128]{3,1,2,0:T(8,128)(2,1)} %bitcast.164) | data formatting | bytes 67108864
  1372.7 29.8 %fusion.64 = f32[4096,1,128]{2,1,0:T(1,128)S(1)} fusion(f32[32,4096,1]{0,2,1:T(1,128)S(1)} %bitcast.177, bf16[32,128,4096]{1,0,2:T(8,128)(2,1)} %bitcast.165), kind=kOutput, calls=%fused_computation.96 | convolution fusion | flops 201326592 | bytes 36175872 | tf_op jit(solution)/shard_map/ksi,ki->si/dot_general | solution.py:113
  1405.4 2.4 copy.39
  1407.8 2.3 fusion.41
  (129 shorter events, 58.9 us)
Async XLA Ops:
  7.2 793.8 %copy-start = (bf16[1,128,2048]{2,1,0:T(8,128)(2,1)S(1)}, bf16[1,128,2048]{2,1,0:T(8,128)(2,1)}, u32[]{:S(2)}) copy-start(bf16[1,128,2048]{2,1,0:T(8,128)(2,1)} %param.15) | copy-start | bytes 1572868
  7.2 793.8 %all-gather.5.cloned.1.call-start = ((), (), s32[]{:S(2)}) async-start(), calls=%async_computation.1 | async-start | bytes 16908288 | tf_op jit(solution)/shard_map/all_gather | solution.py:120
  9.1 2.0 copy-start.8
  10.7 2.1 copy-start.2
  38.5 1272.7 %all-to-all-start = ((f32[32,1,128,4096]{3,2,1,0:T(8,128)}), f32[32,1,128,4096]{3,2,1,0:T(8,128)}, u32[]{:S(2)}, u32[]{:S(2)}) async-start(f32[32,1,128,4096]{3,2,1,0:T(8,128)} %stack.3), calls=%async_computation | async-start | bytes 134217728 | tf_op jit(solution)/shard_map/all_to_all | solution.py:14
  48.0 1301.6 %all-gather.7.cloned.1.call-start = ((), (), s32[]{:S(2)}) async-start(), calls=%async_computation.2 | async-start | bytes 34603008 | tf_op jit(solution)/shard_map/all_gather | solution.py:129
  51.6 761.8 %copy-start.7 = (bf16[1,128,128]{2,1,0:T(8,128)(2,1)S(1)}, bf16[1,128,128]{2,1,0:T(8,128)(2,1)}, u32[]{:S(2)}) copy-start(bf16[1,128,128]{2,1,0:T(8,128)(2,1)} %param.12) | copy-start | bytes 98308
  1372.7 31.2 %copy-start.3 = (f32[128,4096]{0,1:T(8,128)S(1)}, f32[128,4096]{0,1:T(8,128)}, u32[]{:S(2)}) copy-start(f32[128,4096]{0,1:T(8,128)} %get-tuple-element.142) | copy-start | bytes 6291460
  1372.7 31.2 %copy-start.6 = (f32[8,128,8,64]{1,3,2,0:T(8,128)S(1)}, f32[8,128,8,64]{1,3,2,0:T(8,128)}, u32[]{:S(2)}) copy-start(f32[8,128,8,64]{1,3,2,0:T(8,128)} %get-tuple-element.77) | copy-start | bytes 6291460
  1402.6 1.3 copy-start.4
  1405.4 2.4 copy-start.5
  1405.4 4.7 copy-start.1
Sparse Core Ops, SparseCore 0:
  11.1 789.8 all-gather.4
  816.2 272.0 all-gather.6
